TPU v7x, 256 devices: a whole 4x4x8 slice. The times are simulated.
256 devices in a mesh: wide: 16 (over z_lo, x, core), long: 16 (over y, z_hi).
Axes of the slice: x: 4, y: 4, z: 8 (z_hi: 4, z_lo: 2; z = z_hi * 2 + z_lo), core: 2. Of those that a mesh axis runs over, the one named last changes fastest.
Arguments:
- slab_vertices: float32 [3, 4096], P(None, 'wide'), may hold values from 0 to 1
- slab_elements: int32 [3, 8192], P(None, 'wide'), may hold values from 0 to 4095, as said below
- source_vertices: float32 [3, 16384], P(None, ('wide', 'long')), may hold values from 0 to 1
- source_elements: int32 [3, 32768], P(None, ('wide', 'long')), may hold values from 0 to 16383, as said below
- primal_basis: bfloat16 [32, 32768], P(None, ('wide', 'long')), may hold values from -12 to 12
- adjoint_basis: bfloat16 [32, 8192], P(None, 'wide'), may hold values from -24 to 24
Outputs:
- primal_image: float32 [32, 8192], P(None, ('wide', 'long'))
- adjoint_image: float32 [32, 32768], P(None, ('wide', 'long'))
Inputs may be any that keep to these rules, and one draw needn't show every extreme that they name: `slab_elements`: a slab triangle in columns b * 512 to (b + 1) * 512 - 1 names only vertices b * 256 to (b + 1) * 256 - 1; both ends of each such range are named. `source_elements`: a source triangle in columns b * 128 to (b + 1) * 128 - 1 names only vertices b * 64 to (b + 1) * 64 - 1; both ends of each such range are named.
All inputs are finite; a program needn't handle non-finite values.
Results may differ from a plain program's by a relative error of at most 0.0029.
Values may be sent and summed in bfloat16 or wider, within the bound.
A program may use at most 64 MiB of HBM per device.

v0:
```python
import math

import jax
import jax.numpy as jnp
from jax import lax
from jax.sharding import PartitionSpec as P

WAVENUMBER = 40.0
SOFTENING = 0.0004
AREA_WEIGHT = 0.05
FOUR_PI = 4.0 * math.pi


def geometry(vertices, elements, anchor):
    local_ids = elements - anchor
    corners = [jnp.take(vertices, local_ids[corner], axis=1) for corner in range(3)]
    centre = (corners[0] + corners[1] + corners[2]) / 3.0
    edge_one = corners[1] - corners[0]
    edge_two = corners[2] - corners[0]
    normal_x = edge_one[1] * edge_two[2] - edge_one[2] * edge_two[1]
    normal_y = edge_one[2] * edge_two[0] - edge_one[0] * edge_two[2]
    normal_z = edge_one[0] * edge_two[1] - edge_one[1] * edge_two[0]
    areas = 0.5 * jnp.sqrt(normal_x * normal_x + normal_y * normal_y + normal_z * normal_z)
    return jnp.concatenate([centre, areas[None, :]], axis=0)


def kernel_tile(targets, sources):
    spread = targets[0][:, None] - sources[0][None, :]
    square_sum = spread * spread
    for axis_id in range(1, 3):
        spread = targets[axis_id][:, None] - sources[axis_id][None, :]
        square_sum = square_sum + spread * spread
    radius = jnp.sqrt(
        square_sum + SOFTENING + AREA_WEIGHT * (targets[3][:, None] + sources[3][None, :])
    )
    weight = targets[3][:, None] * sources[3][None, :] / (FOUR_PI * radius)
    phases = WAVENUMBER * radius
    return (
        (weight * jnp.cos(phases)).astype(jnp.bfloat16),
        (weight * jnp.sin(phases)).astype(jnp.bfloat16),
    )


def pack_primal(columns):
    half_rows = columns.shape[0] // 2
    real_part = columns[:half_rows]
    imag_part = columns[half_rows:]
    return jnp.concatenate(
        [jnp.concatenate([real_part, -imag_part], 1), jnp.concatenate([imag_part, real_part], 1)], 0
    )


def pack_adjoint(row_block):
    half_rows = row_block.shape[0] // 2
    real_part = row_block[:half_rows]
    imag_part = row_block[half_rows:]
    return jnp.concatenate(
        [jnp.concatenate([real_part, imag_part], 1), jnp.concatenate([imag_part, -real_part], 1)], 0
    )


def primal_part(primal_pack, tile_real, tile_imag):
    stacked = jnp.concatenate([tile_real, tile_imag], 1)
    return lax.dot_general(
        primal_pack, stacked, (((1,), (1,)), ((), ())), preferred_element_type=jnp.float32
    )


def adjoint_part(adjoint_pack, tile_real, tile_imag):
    stacked = jnp.concatenate([tile_real, tile_imag], 0)
    return jnp.dot(adjoint_pack, stacked, preferred_element_type=jnp.float32)


def shards(
    slab_vertices, slab_elements, source_vertices, source_elements, primal_basis, adjoint_basis
):
    slab_width = slab_elements.shape[1]
    source_width = source_elements.shape[1]
    out_rows = primal_basis.shape[0]
    wide_at = lax.axis_index("wide")
    flat_at = wide_at * lax.axis_size("long") + lax.axis_index("long")
    slab_points = geometry(slab_vertices, slab_elements, wide_at * (slab_width // 2))
    source_points = geometry(source_vertices, source_elements, flat_at * (source_width // 2))
    all_slab = lax.all_gather(slab_points, "wide", axis=1, tiled=True)
    primal_pack = pack_primal(primal_basis)
    initial = (
        jnp.zeros((out_rows, source_width), jnp.float32),
        jnp.zeros((out_rows, all_slab.shape[1]), jnp.float32),
    )
    portion = lax.all_gather(adjoint_basis, "wide", axis=1, tiled=True)
    extent = portion.shape[1]
    stride = math.gcd(extent, 1024)

    def advance(block, state):
        adjoint_acc, primal_acc = state
        offset = block * stride
        points = lax.dynamic_slice_in_dim(all_slab, offset, stride, 1)
        row_block = lax.dynamic_slice_in_dim(portion, block * stride, stride, 1)
        tile_real, tile_imag = kernel_tile(points, source_points)
        primal_acc = lax.dynamic_update_slice_in_dim(
            primal_acc, primal_part(primal_pack, tile_real, tile_imag), offset, 1
        )
        adjoint_acc = adjoint_acc + adjoint_part(pack_adjoint(row_block), tile_real, tile_imag)
        return (adjoint_acc, primal_acc)

    adjoint_image, primal_acc = lax.fori_loop(0, extent // stride, advance, initial)
    primal_image = lax.psum_scatter(primal_acc, ("wide", "long"), scatter_dimension=1, tiled=True)
    return (primal_image, adjoint_image)


def solution(mesh):
    return jax.shard_map(
        shards,
        mesh=mesh,
        in_specs=(
            P(None, "wide"),
            P(None, "wide"),
            P(None, ("wide", "long")),
            P(None, ("wide", "long")),
            P(None, ("wide", "long")),
            P(None, "wide"),
        ),
        out_specs=(P(None, ("wide", "long")), P(None, ("wide", "long"))),
        check_vma=False,
    )
```

profile of v0, /device:TPU:32, one launch (start us, length us, event | category | flops | bytes accessed | tf_op | source)
XLA Modules:
  0.0 1602.9 jit_solution(10598250876209024342)
XLA Ops:
  7.2 0.7 broadcast_subtract_fusion
  8.0 0.7 broadcast_subtract_fusion.1
  8.8 0.7 slice_negate_fusion
  9.5 0.8 copy.36
  11.0 0.7 gather_fusion.4
  11.7 0.7 gather_fusion.3
  12.4 0.8 copy.30
  13.3 1.0 gather_fusion.2
  14.4 1.0 gather_fusion.1
  15.6 1.0 gather_fusion
  16.8 18.6 %all_gather.7 = f32[4,8192]{1,0:T(4,128)S(1)} all-gather(f32[4,512]{1,0:T(4,128)S(1)} %pad_maximum_fusion), channel_id=1, replica_groups=mesh['wide'=16,'long'=16] {'wide'}, dimensions={1}, use_global_device_ids=true | all-gather | bytes 139264 | tf_op jit(solution)/shard_map/all_gather | solution.py:84
  35.4 17.9 %all_gather.6 = bf16[32,8192]{1,0:T(8,128)(2,1)S(1)} all-gather(bf16[32,512]{1,0:T(8,128)(2,1)} %param.17), channel_id=1, replica_groups=mesh['wide'=16,'long'=16] {'wide'}, dimensions={1}, use_global_device_ids=true | all-gather | bytes 557056 | tf_op jit(solution)/shard_map/all_gather | solution.py:90
  53.4 29.8 %while.16 = (s32[]{:T(128)}, f32[32,128]{1,0:T(8,128)S(1)}, f32[32,8192]{1,0:T(8,128)S(1)}, bf16[32,8192]{1,0:T(8,128)(2,1)S(1)}, f32[4,8192]{1,0:T(4,128)S(1)},...) while((s32[]{:T(128)}, f32[32,128]{1,0:T(8,128)S(1)}, ...), condition=%wide.region_1.4_spmd.clone, body=%wide.region_0.3_spmd.clone.sunk | while | flops 38854664 | bytes 2069793 | solution.py:106
  53.6 3.1 multiply_convert_fusion.3
  57.3 3.1 multiply_convert_fusion.3
  61.0 3.1 multiply_convert_fusion.3
  64.8 3.1 multiply_convert_fusion.3
  68.5 3.1 multiply_convert_fusion.3
  72.2 3.1 multiply_convert_fusion.3
  75.9 3.1 multiply_convert_fusion.3
  79.6 3.1 multiply_convert_fusion.3
  83.2 2.7 copy.42
  85.9 1508.7 %reduce-scatter.4.cloned.1.call-done = f32[32,32]{1,0:T(8,128)} async-done(((f32[8192,32]{1,0:T(8,128)}), f32[32,32]{1,0:T(8,128)}) %reduce-scatter.4.cloned.1.call-update) | async-done | bytes 4112
  1594.6 1.4 copy.43
  (71 shorter events, 6.2 us)
Async XLA Ops:
  7.2 1587.5 %reduce-scatter.4.cloned.1.call-start = ((), (), s32[]{:S(2)}) async-start(), calls=%async_computation.1 | async-start | bytes 4210688
  83.2 2.7 copy-start
Sparse Core Ops, SparseCore 0:
  86.0 1508.5 reduce-scatter.3
where the time goes:
time: 1600 us
  waiting for transfers between devices  1510 us (94%)
  blocking collectives  36.5 us (2%)
  other arithmetic  27.1 us (2%)
    unnamed x2, waiting for transfers between devices  1510 us
  transfers between devices with their start and end apart: 1, of which 1 were waited for; matrix products, arithmetic and copies ran while one was open for 0% of the time, Pallas kernels for 0%

commit v1 on v0

--- a/solution.py
+++ b/solution.py
@@ -76,35 +76,17 @@
 ):
     slab_width = slab_elements.shape[1]
     source_width = source_elements.shape[1]
-    out_rows = primal_basis.shape[0]
     wide_at = lax.axis_index("wide")
     flat_at = wide_at * lax.axis_size("long") + lax.axis_index("long")
     slab_points = geometry(slab_vertices, slab_elements, wide_at * (slab_width // 2))
     source_points = geometry(source_vertices, source_elements, flat_at * (source_width // 2))
-    all_slab = lax.all_gather(slab_points, "wide", axis=1, tiled=True)
-    primal_pack = pack_primal(primal_basis)
-    initial = (
-        jnp.zeros((out_rows, source_width), jnp.float32),
-        jnp.zeros((out_rows, all_slab.shape[1]), jnp.float32),
-    )
-    portion = lax.all_gather(adjoint_basis, "wide", axis=1, tiled=True)
-    extent = portion.shape[1]
-    stride = math.gcd(extent, 1024)
-
-    def advance(block, state):
-        adjoint_acc, primal_acc = state
-        offset = block * stride
-        points = lax.dynamic_slice_in_dim(all_slab, offset, stride, 1)
-        row_block = lax.dynamic_slice_in_dim(portion, block * stride, stride, 1)
-        tile_real, tile_imag = kernel_tile(points, source_points)
-        primal_acc = lax.dynamic_update_slice_in_dim(
-            primal_acc, primal_part(primal_pack, tile_real, tile_imag), offset, 1
-        )
-        adjoint_acc = adjoint_acc + adjoint_part(pack_adjoint(row_block), tile_real, tile_imag)
-        return (adjoint_acc, primal_acc)
-
-    adjoint_image, primal_acc = lax.fori_loop(0, extent // stride, advance, initial)
-    primal_image = lax.psum_scatter(primal_acc, ("wide", "long"), scatter_dimension=1, tiled=True)
+    gathered_points = lax.all_gather(source_points, "wide", axis=1, tiled=True)
+    gathered_basis = lax.all_gather(primal_basis, "wide", axis=1, tiled=True)
+    tile_real, tile_imag = kernel_tile(slab_points, gathered_points)
+    primal_acc = primal_part(pack_primal(gathered_basis), tile_real, tile_imag)
+    adjoint_acc = adjoint_part(pack_adjoint(adjoint_basis), tile_real, tile_imag)
+    primal_image = lax.psum_scatter(primal_acc, "long", scatter_dimension=1, tiled=True)
+    adjoint_image = lax.psum_scatter(adjoint_acc, "wide", scatter_dimension=1, tiled=True)
     return (primal_image, adjoint_image)
 
 

time: 1600 us -> 233 us (0.15)
  waiting for transfers between devices: 1510 us -> 145 us
    unnamed x2 -> x3, waiting for transfers between devices: 1510 us -> 83.6 us
    reduce_scatter x0 -> x1, waiting for transfers between devices: none -> 61.8 us  [shards(): lax.psum_scatter(adjoint_acc, 'wide', scatter_dimension=1, tiled=True)]
  transfers between devices with their start and end apart: 1 -> 2, of which waited for: 1 -> 2; matrix products, arithmetic and copies ran while one was open for 0% -> 2% of each run, Pallas kernels for 0% -> 0%
where the time goes in v1:
time: 233 us; the launch traced here: 231 us
  waiting for transfers between devices  145 us (62%)
  blocking collectives  35.1 us (15%)
  other arithmetic  20.8 us (9%)
  between operations  14.2 us (6%)
  local copies, waits for them, and re-layouts  9.95 us (4%)
  matrix products  5.05 us (2%)
    unnamed x3, waiting for transfers between devices  83.6 us
    reduce_scatter x1, waiting for transfers between devices, shards(): lax.psum_scatter(adjoint_acc, 'wide', scatter_dimension=1, tiled=True)  61.8 us
    convert_element_type x1, other arithmetic, kernel_tile(): (weight * jnp.cos(phases)).astype(jnp.bfloat16)  19.3 us
    all_gather x1, blocking collectives, shards(): gathered_points = lax.all_gather(source_points, 'wide', axis=1, tiled=True)  18.3 us
    all_gather x1, blocking collectives, shards(): gathered_basis = lax.all_gather(primal_basis, 'wide', axis=1, tiled=True)  16.9 us
    gather x12, local copies, waits for them, and re-layouts, geometry(): jnp.take(vertices, local_ids[corner], axis=1)  5.6 us
  transfers between devices with their start and end apart: 2, of which 2 were waited for; matrix products, arithmetic and copies ran while one was open for 2% of the time, Pallas kernels for 0%

profile of v1, /device:TPU:32, one launch (start us, length us, event | category | flops | bytes accessed | tf_op | source)
XLA Modules:
  0.0 230.7 jit_solution(14007705249488354865)
XLA Ops:
  7.2 0.7 broadcast_subtract_fusion
  8.0 0.8 copy.35
  8.8 0.7 broadcast_subtract_fusion.1
  9.5 0.6 gather_fusion.5
  10.1 0.1 copy.40
  10.2 0.7 gather_fusion.4
  10.9 0.1 copy.38
  10.9 0.7 gather_fusion.3
  11.7 18.3 %all_gather.7 = f32[4,2048]{1,0:T(4,128)S(1)} all-gather(f32[4,128]{1,0:T(4,128)S(1)} %pad_maximum_fusion), channel_id=1, replica_groups=mesh['wide'=16,'long'=16] {'wide'}, dimensions={1}, use_global_device_ids=true | all-gather | bytes 34816 | tf_op jit(solution)/shard_map/all_gather | solution.py:83
  30.0 0.8 copy.29
  30.9 1.0 gather_fusion.2
  31.9 0.1 copy.34
  32.0 1.0 gather_fusion.1
  33.1 0.1 copy.32
  33.2 1.0 gather_fusion
  34.2 0.1 copy.30
  34.4 16.9 %all_gather.6 = bf16[32,2048]{1,0:T(8,128)(2,1)S(1)} all-gather(bf16[32,128]{1,0:T(8,128)(2,1)} %param.14), channel_id=1, replica_groups=mesh['wide'=16,'long'=16] {'wide'}, dimensions={1}, use_global_device_ids=true | all-gather | bytes 139264 | tf_op jit(solution)/shard_map/all_gather | solution.py:84
  51.3 19.3 %multiply_convert_fusion.1 = (bf16[512,2048]{1,0:T(8,128)(2,1)S(1)}, bf16[512,2048]{1,0:T(8,128)(2,1)S(1)}) fusion(f32[2048]{0:T(1024)S(1)} %bitcast.59, f32[512]{0:T(512)S(1)} %bitcast.64, f32[2048]{0:T(1024)S(1)} %bitcast.60, f32[512]{0:T(512)S(1)} %bitcast.65, f32[2048]{0:T(1024)S(1)} %bitcast.61, f32[512]{0:T(512)S(1)} %bitcast.63, ...), kind=kLoop, calls=%fused_computation.15 | loop fusion | flops 20971520 | bytes 4235264 | tf_op jit(solution)/shard_map/convert_element_type | solution.py:39
  70.6 1.3 copy-done.1
  71.9 1.9 fusion.8
  73.9 3.1 %fusion.4 = f32[32,2048]{1,0:T(8,128)} fusion(bf16[512,2048]{1,0:T(8,128)(2,1)} %copy-done.1, bf16[512,2048]{1,0:T(8,128)(2,1)S(1)} %get-tuple-element.13, bf16[16,512]{1,0:T(8,128)(2,1)S(1)} %get-tuple-element.16, bf16[16,512]{1,0:T(8,128)(2,1)S(1)} %get-tuple-element.17, bf16[16,512]{1,0:T(8,128)(2,1)S(1)} %get-tuple-element.15), kind=kOutput, calls=%fused_computation.10 | convolution fusion | flops 142868480 | bytes 4505600 | tf_op jit(solution)/shard_map/dot_general | solution.py:71
  77.1 83.6 %reduce-scatter.7.cloned.1.call-done = f32[32,32]{1,0:T(8,128)} async-done(((f32[512,32]{1,0:T(8,128)}), f32[32,32]{1,0:T(8,128)}) %reduce-scatter.7.cloned.1.call-update) | async-done | bytes 4112
  160.6 1.4 copy.42
  162.0 61.8 %reduce-scatter.5.cloned.1.call-done = f32[32,128]{1,0:T(8,128)} async-done(((f32[32,2048]{1,0:T(8,128)}), f32[32,128]{1,0:T(8,128)}) %reduce-scatter.5.cloned.1.call-update) | async-done | bytes 16400 | tf_op jit(solution)/shard_map/reduce_scatter | solution.py:89
  (29 shorter events, 0.4 us)
Async XLA Ops:
  7.2 153.5 %reduce-scatter.7.cloned.1.call-start = ((), (), s32[]{:S(2)}) async-start(), calls=%async_computation.3 | async-start | bytes 278528
  70.6 1.3 copy-start.1
  71.9 2.0 copy-start
  73.8 150.0 %reduce-scatter.5.cloned.1.call-start = ((), (), s32[]{:S(2)}) async-start(), calls=%async_computation.2 | async-start | bytes 278528 | tf_op jit(solution)/shard_map/reduce_scatter | solution.py:89
Sparse Core Ops, SparseCore 0:
  74.0 86.6 reduce-scatter.6
  163.8 59.9 reduce-scatter.4
